TPU v7x, 256 devices: a whole 4x4x8 slice. The times are simulated.
256 devices in a mesh: gx: 8 (over y, core), gy: 32 (over x, z).
Axes of the slice: x: 4, y: 4, z: 8, core: 2. Of those that a mesh axis runs over, the one named last changes fastest.
Arguments:
- projected: bfloat16 [32, 512, 3072], P('gx', 'gy'), may hold values from -8 to 8
- residual: bfloat16 [32, 512, 1024], P('gx', 'gy'), may hold values from -6 to 6
- page_store: bfloat16 [256, 72, 128, 256], P(('gx', 'gy')), may hold values from -8 to 8
- page_table: int32 [32, 64], P('gx'), may hold values from 0 to 71, as said below
- lengths: int32 [32], P('gx'), may hold values from 1 to 8192, as said below
- persistent: bfloat16 [2, 16, 1024], replicated, may hold values from -8 to 8
- memory_rates: float32 [256, 3, 8], P(('gx', 'gy')), may hold values from 0.002 to 0.95
- memory_state: float32 [256, 128, 128], P(('gx', 'gy')), may hold values from -6 to 6
- momentum: float32 [256, 128, 128], P(('gx', 'gy')), may hold values from -2 to 2
- w_out: bfloat16 [1024, 1024], P('gy', 'gx'), may hold values from -0.1875 to 0.1875
Outputs:
- layer_out: bfloat16 [32, 512, 1024], P('gx', 'gy')
- memory_next: float32 [256, 128, 128], P(('gx', 'gy'))
- momentum_next: float32 [256, 128, 128], P(('gx', 'gy'))
Inputs may be any that keep to these rules, and one draw needn't show every extreme that they name: `page_table`: the 64 entries of a request's row are distinct slots. `lengths`: some request has exactly 8192 cached tokens.
All inputs are finite; a program needn't handle non-finite values.
Results may differ from a plain program's by a relative error of at most 0.012.
Values may be sent and summed in bfloat16 or wider, within the bound.
No kernel may reach another device: no remote copies, remote signals or barrier semaphores. Data moves between devices by JAX's collectives and lax.ppermute only.
A program may use at most 64 MiB of HBM per device.

v0:
```python
import math
import jax
import jax.numpy as jnp
from jax import lax
from jax.sharding import PartitionSpec as P

D = 1024
HEADS = 8
HD = 128
MB = 64
PAGE = 128
MAXP = 64
NB = 8
masked_score = -1e30


def for_sending(value):

    def short(part):
        return part.astype(jnp.bfloat16) if part.dtype == jnp.float32 else part

    return jax.tree.map(short, value)


def absorb(carried, scores, values):
    running, totals, summed = carried
    newest = jnp.maximum(running, jnp.max(scores, axis=1))
    factor = jnp.exp(running - newest)
    weights = jnp.exp(scores - newest[:, None])
    totals = totals * factor + jnp.sum(weights, axis=1)
    summed = summed * factor[:, None] + jnp.dot(
        weights.astype(jnp.bfloat16), values, preferred_element_type=jnp.float32
    )
    return (newest, totals, summed)


def recall(queries, keyed, valued, rates_here, memory, moment):
    keys_wide = keyed.astype(jnp.float32)
    keys_wide = keys_wide / jnp.sqrt(jnp.sum(keys_wide * keys_wide, axis=1, keepdims=True) + 1e-06)
    query_wide = queries.astype(jnp.float32)
    query_wide = query_wide / jnp.sqrt(
        jnp.sum(query_wide * query_wide, axis=1, keepdims=True) + 1e-06
    )
    values_wide = valued.astype(jnp.float32)
    pieces = []
    for block_id in range(NB):
        start_row = block_id * MB
        key_block = keys_wide[start_row : start_row + MB]
        query_block = query_wide[start_row : start_row + MB]
        value_block = values_wide[start_row : start_row + MB]
        pieces.append(jnp.dot(query_block, memory, precision=lax.Precision.HIGHEST))
        errors = jnp.dot(key_block, memory, precision=lax.Precision.HIGHEST) - value_block
        gradient = jnp.dot(key_block.T, errors, precision=lax.Precision.HIGHEST)
        moment = rates_here[0, block_id] * moment - rates_here[1, block_id] * gradient
        memory = (1.0 - rates_here[2, block_id]) * memory + moment
    return (jnp.concatenate(pieces, 0), memory, moment)


def shards(
    projected,
    residual,
    page_store,
    page_table,
    lengths,
    persistent,
    memory_rates,
    memory_state,
    momentum,
    w_out,
):
    groups, positions, triple = projected.shape
    pair_count = memory_state.shape[0]
    sectioned = (
        projected.reshape(groups, positions, 3, HEADS, HD)
        .transpose(0, 3, 1, 2, 4)
        .reshape(groups * HEADS, positions, 3 * HD)
    )
    paired = lax.all_to_all(sectioned, "gy", split_axis=0, concat_axis=1, tiled=True)
    offset = lax.axis_index("gy") * pair_count
    pages_block = math.gcd(MAXP, max(1, 512 // PAGE))
    key_span = pages_block * PAGE
    scaling = HD ** (-0.5)

    def handle(member):
        ordinal, segment, pages_here, rates_here, memory, moment = member
        within = offset + ordinal
        request = within // HEADS
        head_id = within % HEADS
        table_row = lax.dynamic_index_in_dim(page_table, request, 0, keepdims=False)
        length = lax.dynamic_index_in_dim(lengths, request, 0, keepdims=False)
        pers_keys = lax.dynamic_slice_in_dim(persistent[0], head_id * HD, HD, 1)
        pers_values = lax.dynamic_slice_in_dim(persistent[1], head_id * HD, HD, 1)
        queries = segment[:, :HD]
        keyed = segment[:, HD : 2 * HD]
        valued = segment[:, 2 * HD :]
        row_count = segment.shape[0]
        carried = (
            jnp.full((row_count,), masked_score, jnp.float32),
            jnp.zeros((row_count,), jnp.float32),
            jnp.zeros((row_count, HD), jnp.float32),
        )
        scores = jnp.dot(queries, pers_keys.T, preferred_element_type=jnp.float32) * scaling
        carried = absorb(carried, scores, pers_values)

        def visit_block(block_id, carried):
            first_page = block_id * pages_block
            fetched_pages = []
            for within_block in range(pages_block):
                slot_here = lax.dynamic_index_in_dim(
                    table_row, first_page + within_block, 0, keepdims=False
                )
                fetched_pages.append(
                    lax.dynamic_index_in_dim(pages_here, slot_here, 0, keepdims=False)
                )
            fetched = jnp.concatenate(fetched_pages, 0)
            key_pos = block_id * key_span + jnp.arange(key_span, dtype=jnp.int32)
            scores = (
                jnp.dot(queries, fetched[:, :HD].T, preferred_element_type=jnp.float32) * scaling
            )
            scores = jnp.where((key_pos < length)[None, :], scores, masked_score)
            return absorb(carried, scores, fetched[:, HD:])

        block_count = MAXP // pages_block
        carried = lax.fori_loop(0, block_count, visit_block, carried)
        places = jnp.arange(row_count, dtype=jnp.int32)
        causal = places[None, :] <= places[:, None]
        scores = jnp.dot(queries, keyed.T, preferred_element_type=jnp.float32) * scaling
        scores = jnp.where(causal, scores, masked_score)
        newest, totals, summed = absorb(carried, scores, valued)
        attended = summed / totals[:, None]
        recalled, memory, moment = recall(queries, keyed, valued, rates_here, memory, moment)
        mixed = (attended + recalled).astype(jnp.bfloat16)
        return (mixed, memory, moment)

    mixed, memory_next, momentum_next = lax.map(
        handle,
        (
            jnp.arange(pair_count, dtype=jnp.int32),
            paired,
            page_store,
            memory_rates,
            memory_state,
            momentum,
        ),
    )
    returned = jax.tree.map(
        lambda part, own: part.astype(own.dtype),
        lax.all_to_all(for_sending(mixed), "gy", split_axis=1, concat_axis=0, tiled=True),
        mixed,
    )
    tokens_here = (
        returned.reshape(groups, HEADS, positions, HD)
        .transpose(0, 2, 1, 3)
        .reshape(groups, positions, D)
    )
    wide_rows = lax.all_gather(w_out, "gx", axis=1, tiled=True)
    flattened = tokens_here.reshape(groups * positions, D)
    weight_piece = lax.all_gather(wide_rows, "gy", axis=0, tiled=True)
    taken = lax.slice_in_dim(flattened, 0, weight_piece.shape[0], axis=1)
    product = jnp.zeros((groups * positions, D), jnp.float32) + jnp.dot(
        taken, weight_piece, preferred_element_type=jnp.float32
    )
    layer_out = (
        (residual.reshape(groups * positions, D).astype(jnp.float32) + product)
        .astype(jnp.bfloat16)
        .reshape(groups, positions, D)
    )
    return (layer_out, memory_next, momentum_next)


def solution(mesh):
    in_specs = (
        P("gx", "gy", None),
        P("gx", "gy", None),
        P(("gx", "gy"), None, None, None),
        P("gx", None),
        P("gx"),
        P(),
        P(("gx", "gy"), None, None),
        P(("gx", "gy"), None, None),
        P(("gx", "gy"), None, None),
        P("gy", "gx"),
    )
    out_specs = (P("gx", "gy", None), P(("gx", "gy"), None, None), P(("gx", "gy"), None, None))
    return jax.shard_map(shards, mesh=mesh, in_specs=in_specs, out_specs=out_specs, check_vma=False)
```

profile of v0, /device:TPU:8, one launch (start us, length us, event | category | flops | bytes accessed | tf_op | source)
XLA Modules:
  0.0 270.0 jit_solution(14022602897338889470)
XLA Ops:
  7.2 1.1 copy.24
  8.6 1.1 reshape.79
  9.7 11.4 %all-to-all-start = ((bf16[32,16,384]{2,1,0:T(8,128)(2,1)}), bf16[32,16,384]{2,1,0:T(8,128)(2,1)S(1)}, u32[]{:S(2)}, u32[]{:S(2)}) async-start(bf16[32,16,384]{2,1,0:T(8,128)(2,1)} %reshape.79), calls=%async_computation | async-start | bytes 786432 | tf_op jit(solution)/shard_map/all_to_all | solution.py:78
  21.2 12.8 %all_gather.6 = bf16[32,1024]{1,0:T(8,128)(2,1)} all-gather(bf16[32,128]{1,0:T(8,128)(2,1)S(1)} %copy-done.6), channel_id=1, replica_groups=mesh['gx'=8,'gy'=32] {'gx'}, dimensions={1}, use_global_device_ids=true | all-gather | bytes 73728 | tf_op jit(solution)/shard_map/all_gather | solution.py:156
  42.2 1.5 fusion.33
  43.9 1.6 multiply_add_fusion.6
  46.2 180.2 %while.30 = (s32[]{:T(128)}, f32[512]{0:T(512)S(1)}, f32[512]{0:T(512)S(1)}, f32[512,128]{1,0:T(8,128)S(1)}, s32[]{:T(128)}, /*index=5*/s32[64]{0:T(128)S(1)}, b...) while((s32[]{:T(128)}, f32[512]{0:T(512)S(1)}, ...), condition=%wide.region_5.6_spmd, body=%wide.region_2.5_spmd.sunk | while | flops 137234464 | bytes 5146177 | solution.py:124
  54.7 1.0 dynamic-slice_bitcast_fusion.5
  66.0 1.0 dynamic-slice_bitcast_fusion.5
  88.5 1.0 dynamic-slice_bitcast_fusion.5
  111.1 1.0 dynamic-slice_bitcast_fusion.5
  122.3 1.0 dynamic-slice_bitcast_fusion.5
  144.9 1.0 dynamic-slice_bitcast_fusion.5
  178.6 1.0 dynamic-slice_bitcast_fusion.5
  227.1 1.5 multiply_add_fusion.5
  229.0 1.5 multiply_add_fusion.4
  230.9 1.6 multiply_add_fusion.3
  232.8 1.4 multiply_add_fusion.2
  234.6 1.5 multiply_add_fusion.1
  237.4 1.4 reduce.4
  239.6 9.8 %all-to-all-start.1 = ((bf16[32,2,1024]{2,1,0:T(2,128)(2,1)}), bf16[32,2,1024]{2,1,0:T(2,128)(2,1)S(1)}, u32[]{:S(2)}, u32[]{:S(2)}) async-start(bf16[32,2,1024]{2,1,0:T(2,128)(2,1)} %reshape.83), calls=%async_computation.1 | async-start | bytes 262144 | tf_op jit(solution)/shard_map/all_to_all | solution.py:148
  249.6 1.5 fusion.13
  251.8 8.4 %all-to-all-done.1 = bf16[32,2,1024]{2,1,0:T(2,128)(2,1)S(1)} async-done(((bf16[32,2,1024]{2,1,0:T(2,128)(2,1)}), bf16[32,2,1024]{2,1,0:T(2,128)(2,1)S(1)}, u32[]{:S(2)}, u32[]{:S(2)}) %all-to-all-start.1) | async-done | bytes 131104 | tf_op jit(solution)/shard_map/all_to_all | solution.py:148
  260.4 2.7 %fusion.10 = bf16[64,1024]{1,0:T(8,128)(2,1)} fusion(bf16[1024,1024]{1,0:T(8,128)(2,1)} %all-gather.2.cloned.1.call-done, bf16[64,1024]{1,0:T(8,128)(2,1)S(1)} %bitcast.140, bf16[8,8,8,128]{3,2,1,0:T(8,128)(2,1)S(1)} %bitcast.135), kind=kOutput, calls=%fused_computation.24 | convolution fusion | flops 134414336 | bytes 2490368 | tf_op jit(solution)/shard_map/dot_general | solution.py:160
  (219 shorter events, 55.4 us)
Async XLA Ops:
  7.2 34.0 %copy-start = (s32[4,64]{1,0:T(4,128)S(1)}, s32[4,64]{1,0:T(4,128)}, u32[]{:S(2)}) copy-start(s32[4,64]{1,0:T(4,128)} %param.15) | copy-start | bytes 3076
  7.2 14.0 %copy-start.6 = (bf16[32,128]{1,0:T(8,128)(2,1)S(1)}, bf16[32,128]{1,0:T(8,128)(2,1)}, u32[]{:S(2)}) copy-start(bf16[32,128]{1,0:T(8,128)(2,1)} %param.21) | copy-start | bytes 24580
  7.2 26.9 %copy-start.7 = (f32[1,3,8]{2,0,1:T(1,128)S(1)}, f32[1,3,8]{2,0,1:T(1,128)}, u32[]{:S(2)}) copy-start(f32[1,3,8]{2,0,1:T(1,128)} %param.18) | copy-start | bytes 292
  7.2 33.2 %copy-start.8 = (s32[4]{0:T(128)S(1)}, s32[4]{0:T(128)}, u32[]{:S(2)}) copy-start(s32[4]{0:T(128)} %param.16) | copy-start | bytes 52
  7.2 33.9 %copy-start.5 = (bf16[2,16,1024]{2,1,0:T(8,128)(2,1)S(1)}, bf16[2,16,1024]{2,1,0:T(8,128)(2,1)}, u32[]{:S(2)}) copy-start(bf16[2,16,1024]{2,1,0:T(8,128)(2,1)} %param.17) | copy-start | bytes 196612
  9.7 32.3 %copy-start.1 = (f32[1,128,128]{2,1,0:T(8,128)S(1)}, f32[1,128,128]{2,1,0:T(8,128)}, u32[]{:S(2)}) copy-start(f32[1,128,128]{2,1,0:T(8,128)} %param.19) | copy-start | bytes 196612
  9.7 31.5 %all-to-all-start = ((bf16[32,16,384]{2,1,0:T(8,128)(2,1)}), bf16[32,16,384]{2,1,0:T(8,128)(2,1)S(1)}, u32[]{:S(2)}, u32[]{:S(2)}) async-start(bf16[32,16,384]{2,1,0:T(8,128)(2,1)} %reshape.79), calls=%async_computation | async-start | bytes 786432 | tf_op jit(solution)/shard_map/all_to_all | solution.py:78
  21.1 21.0 %copy-start.4 = (f32[1,128,128]{2,1,0:T(8,128)S(1)}, f32[1,128,128]{2,1,0:T(8,128)}, u32[]{:S(2)}) copy-start(f32[1,128,128]{2,1,0:T(8,128)} %param.20) | copy-start | bytes 196612
  21.1 239.2 %all-gather.2.cloned.1.call-start = ((), (), s32[]{:S(2)}) async-start(), calls=%async_computation.2 | async-start | bytes 2162688 | tf_op jit(solution)/shard_map/all_gather | solution.py:158
  236.3 24.1 %copy-start.3 = (bf16[4,16,1024]{2,1,0:T(8,128)(2,1)S(1)}, bf16[4,16,1024]{2,1,0:T(8,128)(2,1)}, u32[]{:S(2)}) copy-start(bf16[4,16,1024]{2,1,0:T(8,128)(2,1)} %param.13) | copy-start | bytes 393220
  239.6 20.6 %all-to-all-start.1 = ((bf16[32,2,1024]{2,1,0:T(2,128)(2,1)}), bf16[32,2,1024]{2,1,0:T(2,128)(2,1)S(1)}, u32[]{:S(2)}, u32[]{:S(2)}) async-start(bf16[32,2,1024]{2,1,0:T(2,128)(2,1)} %reshape.83), calls=%async_computation.1 | async-start | bytes 262144 | tf_op jit(solution)/shard_map/all_to_all | solution.py:148
  251.1 12.0 %copy-start.2 = (f32[128,128]{1,0:T(8,128)}, f32[128,128]{1,0:T(8,128)S(1)}, u32[]{:S(2)}) copy-start(f32[128,128]{1,0:T(8,128)S(1)} %fusion.13) | copy-start | bytes 196612
Sparse Core Ops, SparseCore 0:
  34.2 78.4 all-gather.1
where the time goes:
time: 273 us; the launch traced here: 270 us
  loops' own time  127 us (47%)
  local copies, waits for them, and re-layouts  32.4 us (12%)
  matrix products  30.3 us (11%)
  starting transfers between devices  21.3 us (8%)
  between operations  19.5 us (7%)
  other arithmetic  17.8 us (7%)
  blocking collectives  12.8 us (5%)
  waiting for transfers between devices  8.45 us (3%)
    another operation x1, loops' own time, handle(): carried = lax.fori_loop(0, block_count, visit_block, carried)  127 us
    squeeze x16, local copies, waits for them, and re-layouts, visit_block(): lax.dynamic_index_in_dim(pages_here, slot_here, 0, keepdims=False)  15.4 us
    all_gather x1, blocking collectives, shards(): wide_rows = lax.all_gather(w_out, 'gx', axis=1, tiled=True)  12.8 us
    dot_general x8, matrix products, recall(): gradient = jnp.dot(key_block.T, errors, precision=lax.Precision.HIGHEST)  12.1 us
    all_to_all x1, starting transfers between devices, shards(): lax.all_to_all(sectioned, 'gy', split_axis=0, concat_axis=1, tiled=True)  11.4 us
    lt x16, other arithmetic, visit_block(): scores = jnp.where((key_pos < length)[None, :], scores, masked_score)  11.1 us
    dynamic_slice x16, local copies, waits for them, and re-layouts, visit_block(): lax.dynamic_index_in_dim(table_row, first_page + within_block, 0, keepdim...  10.9 us
    all_to_all x1, starting transfers between devices, shards(): lax.all_to_all(for_sending(mixed), 'gy', split_axis=1, concat_axis=0, til...  9.79 us
  transfers between devices with their start and end apart: 3, of which 1 were waited for; matrix products, arithmetic and copies ran while one was open for 28% of the time, Pallas kernels for 0%

commit v1 on v0

--- a/solution.py
+++ b/solution.py
@@ -155,7 +155,9 @@
     )
     wide_rows = lax.all_gather(w_out, "gx", axis=1, tiled=True)
     flattened = tokens_here.reshape(groups * positions, D)
-    weight_piece = lax.all_gather(wide_rows, "gy", axis=0, tiled=True)
+    weight_piece = jnp.concatenate(
+        lax.all_to_all(jnp.stack([wide_rows] * lax.axis_size("gy")), "gy", 0, 0), axis=0
+    )
     taken = lax.slice_in_dim(flattened, 0, weight_piece.shape[0], axis=1)
     product = jnp.zeros((groups * positions, D), jnp.float32) + jnp.dot(
         taken, weight_piece, preferred_element_type=jnp.float32

time: 273 us -> 302 us (1.11)
  waiting for transfers between devices: 8.45 us -> 55.4 us
  between operations: 19.5 us -> 6.2 us
  loops' own time: 127 us -> 119 us
  starting transfers between devices: 21.3 us -> 26.4 us
    all_to_all x0 -> x1, waiting for transfers between devices: none -> 47.4 us  [shards(): lax.all_to_all(jnp.stack([wide_rows] * lax.axis_size('gy')), 'gy', 0, 0)]
    all_to_all x0 -> x1, starting transfers between devices: none -> 9.92 us  [shards(): lax.all_to_all(jnp.stack([wide_rows] * lax.axis_size('gy')), 'gy', 0, 0)]
    another operation x1, loops' own time: 127 us -> 119 us  [handle(): carried = lax.fori_loop(0, block_count, visit_block, carried)]
    all_to_all x1, waiting for transfers between devices: 8.41 us -> 0.01 us  [shards(): lax.all_to_all(for_sending(mixed), 'gy', split_axis=1, concat_axis=0, til...]
    all_to_all x1, waiting for transfers between devices: 0.01 us -> 7.97 us  [shards(): lax.all_to_all(sectioned, 'gy', split_axis=0, concat_axis=1, tiled=True)]
    all_to_all x1, starting transfers between devices: 9.79 us -> 5.13 us  [shards(): lax.all_to_all(for_sending(mixed), 'gy', split_axis=1, concat_axis=0, til...]
  transfers between devices with their start and end apart: 3 -> 3, of which waited for: 1 -> 2; matrix products, arithmetic and copies ran while one was open for 28% -> 1% of each run, Pallas kernels for 0% -> 0%
where the time goes in v1:
time: 302 us; the launch traced here: 299 us
  loops' own time  119 us (39%)
  waiting for transfers between devices  55.4 us (18%)
  local copies, waits for them, and re-layouts  33.9 us (11%)
  matrix products  30.1 us (10%)
  starting transfers between devices  26.4 us (9%)
  other arithmetic  16.4 us (5%)
  blocking collectives  11.7 us (4%)
  between operations  6.2 us (2%)
    another operation x1, loops' own time, handle(): carried = lax.fori_loop(0, block_count, visit_block, carried)  119 us
    all_to_all x1, waiting for transfers between devices, shards(): lax.all_to_all(jnp.stack([wide_rows] * lax.axis_size('gy')), 'gy', 0, 0)  47.4 us
    squeeze x16, local copies, waits for them, and re-layouts, visit_block(): lax.dynamic_index_in_dim(pages_here, slot_here, 0, keepdims=False)  15.4 us
    dot_general x8, matrix products, recall(): gradient = jnp.dot(key_block.T, errors, precision=lax.Precision.HIGHEST)  12.6 us
    all_gather x1, blocking collectives, shards(): wide_rows = lax.all_gather(w_out, 'gx', axis=1, tiled=True)  11.7 us
    all_to_all x1, starting transfers between devices, shards(): lax.all_to_all(sectioned, 'gy', split_axis=0, concat_axis=1, tiled=True)  11.3 us
    dynamic_slice x16, local copies, waits for them, and re-layouts, visit_block(): lax.dynamic_index_in_dim(table_row, first_page + within_block, 0, keepdim...  10.8 us
    all_to_all x1, starting transfers between devices, shards(): lax.all_to_all(jnp.stack([wide_rows] * lax.axis_size('gy')), 'gy', 0, 0)  9.92 us
  transfers between devices with their start and end apart: 3, of which 2 were waited for; matrix products, arithmetic and copies ran while one was open for 1% of the time, Pallas kernels for 0%

profile of v1, /device:TPU:8, one launch (start us, length us, event | category | flops | bytes accessed | tf_op | source)
XLA Modules:
  0.0 299.1 jit_solution(12247978605096847188)
XLA Ops:
  0.7 1.1 copy.24
  2.0 1.1 reshape.84
  3.1 11.3 %all-to-all-start = ((bf16[32,16,384]{2,1,0:T(8,128)(2,1)}), bf16[32,16,384]{2,1,0:T(8,128)(2,1)S(1)}, u32[]{:S(2)}, u32[]{:S(2)}) async-start(bf16[32,16,384]{2,1,0:T(8,128)(2,1)} %reshape.84), calls=%async_computation | async-start | bytes 786432 | tf_op jit(solution)/shard_map/all_to_all | solution.py:78
  21.0 8.0 %all-to-all-done = bf16[32,16,384]{2,1,0:T(8,128)(2,1)S(1)} async-done(((bf16[32,16,384]{2,1,0:T(8,128)(2,1)}), bf16[32,16,384]{2,1,0:T(8,128)(2,1)S(1)}, u32[]{:S(2)}, u32[]{:S(2)}) %all-to-all-start) | async-done | bytes 393248 | tf_op jit(solution)/shard_map/all_to_all | solution.py:78
  29.2 1.3 fusion.79
  31.0 170.2 %while.30 = (s32[]{:T(128)}, f32[512]{0:T(512)S(1)}, f32[512]{0:T(512)S(1)}, f32[512,128]{1,0:T(8,128)S(1)}, s32[]{:T(128)}, /*index=5*/s32[64]{0:T(128)S(1)}, b...) while((s32[]{:T(128)}, f32[512]{0:T(512)S(1)}, ...), condition=%wide.region_5.6_spmd, body=%wide.region_2.5_spmd.sunk | while | flops 137234464 | bytes 5146185 | solution.py:124
  50.4 1.0 dynamic-slice_bitcast_fusion.5
  92.9 1.0 dynamic-slice_bitcast_fusion.5
  114.2 1.0 dynamic-slice_bitcast_fusion.5
  201.7 1.6 fusion.33
  203.5 1.7 multiply_add_fusion.6
  205.4 1.6 multiply_add_fusion.5
  207.2 1.5 multiply_add_fusion.4
  208.9 1.5 multiply_add_fusion.3
  210.6 1.6 multiply_add_fusion.2
  213.7 1.6 multiply_add_fusion.1
  216.9 1.4 reduce.4
  219.0 5.1 %all-to-all-start.1 = ((bf16[32,2,1024]{2,1,0:T(2,128)(2,1)}), bf16[32,2,1024]{2,1,0:T(2,128)(2,1)S(1)}, u32[]{:S(2)}, u32[]{:S(2)}) async-start(bf16[32,2,1024]{2,1,0:T(2,128)(2,1)} %reshape.89), calls=%async_computation.1 | async-start | bytes 262144 | tf_op jit(solution)/shard_map/all_to_all | solution.py:148
  224.1 11.7 %all_gather.3 = bf16[32,1024]{1,0:T(8,128)(2,1)S(1)} all-gather(bf16[32,128]{1,0:T(8,128)(2,1)S(1)} %copy-done.7), channel_id=1, replica_groups=mesh['gx'=8,'gy'=32] {'gx'}, dimensions={1}, use_global_device_ids=true | all-gather | bytes 73728 | tf_op jit(solution)/shard_map/all_gather | solution.py:156
  235.9 1.6 stack.2
  237.4 9.9 %all-to-all-start.2 = ((bf16[32,32,1024]{2,1,0:T(8,128)(2,1)}), bf16[32,32,1024]{2,1,0:T(8,128)(2,1)S(1)}, u32[]{:S(2)}, u32[]{:S(2)}) async-start(bf16[32,32,1024]{2,1,0:T(8,128)(2,1)} %stack.2), calls=%async_computation.2 | async-start | bytes 4194304 | tf_op jit(solution)/shard_map/all_to_all | solution.py:159
  248.1 1.5 fusion.13
  250.5 47.4 %all-to-all-done.2 = bf16[32,32,1024]{2,1,0:T(8,128)(2,1)S(1)} async-done(((bf16[32,32,1024]{2,1,0:T(8,128)(2,1)}), bf16[32,32,1024]{2,1,0:T(8,128)(2,1)S(1)}, u32[]{:S(2)}, u32[]{:S(2)}) %all-to-all-start.2) | async-done | bytes 2097184 | tf_op jit(solution)/shard_map/all_to_all | solution.py:159
  297.9 1.1 fusion.10
  (221 shorter events, 57.4 us)
Async XLA Ops:
  0.6 20.4 %copy-start = (s32[4,64]{1,0:T(4,128)S(1)}, s32[4,64]{1,0:T(4,128)}, u32[]{:S(2)}) copy-start(s32[4,64]{1,0:T(4,128)} %param.15) | copy-start | bytes 3076
  0.6 13.8 %copy-start.8 = (f32[1,3,8]{2,0,1:T(1,128)S(1)}, f32[1,3,8]{2,0,1:T(1,128)}, u32[]{:S(2)}) copy-start(f32[1,3,8]{2,0,1:T(1,128)} %param.18) | copy-start | bytes 292
  0.7 19.7 %copy-start.9 = (s32[4]{0:T(128)S(1)}, s32[4]{0:T(128)}, u32[]{:S(2)}) copy-start(s32[4]{0:T(128)} %param.16) | copy-start | bytes 52
  0.7 20.3 %copy-start.6 = (bf16[2,16,1024]{2,1,0:T(8,128)(2,1)S(1)}, bf16[2,16,1024]{2,1,0:T(8,128)(2,1)}, u32[]{:S(2)}) copy-start(bf16[2,16,1024]{2,1,0:T(8,128)(2,1)} %param.17) | copy-start | bytes 196612
  3.1 25.9 %all-to-all-start = ((bf16[32,16,384]{2,1,0:T(8,128)(2,1)}), bf16[32,16,384]{2,1,0:T(8,128)(2,1)S(1)}, u32[]{:S(2)}, u32[]{:S(2)}) async-start(bf16[32,16,384]{2,1,0:T(8,128)(2,1)} %reshape.84), calls=%async_computation | async-start | bytes 786432 | tf_op jit(solution)/shard_map/all_to_all | solution.py:78
  31.0 170.5 %copy-start.2 = (f32[1,128,128]{2,1,0:T(8,128)S(1)}, f32[1,128,128]{2,1,0:T(8,128)}, u32[]{:S(2)}) copy-start(f32[1,128,128]{2,1,0:T(8,128)} %param.19) | copy-start | bytes 196612
  31.0 170.7 %copy-start.5 = (f32[1,128,128]{2,1,0:T(8,128)S(1)}, f32[1,128,128]{2,1,0:T(8,128)}, u32[]{:S(2)}) copy-start(f32[1,128,128]{2,1,0:T(8,128)} %param.20) | copy-start | bytes 196612
  203.3 12.2 %copy-start.1 = (f32[512,512]{0,1:T(8,128)S(1)}, f32[512,512]{0,1:T(8,128)}, u32[]{:S(2)}) copy-start(f32[512,512]{0,1:T(8,128)} %get-tuple-element.338) | copy-start | bytes 3145732
  215.5 8.6 %copy-start.7 = (bf16[32,128]{1,0:T(8,128)(2,1)S(1)}, bf16[32,128]{1,0:T(8,128)(2,1)}, u32[]{:S(2)}) copy-start(bf16[32,128]{1,0:T(8,128)(2,1)} %param.21) | copy-start | bytes 24580
  219.0 16.9 %all-to-all-start.1 = ((bf16[32,2,1024]{2,1,0:T(2,128)(2,1)}), bf16[32,2,1024]{2,1,0:T(2,128)(2,1)S(1)}, u32[]{:S(2)}, u32[]{:S(2)}) async-start(bf16[32,2,1024]{2,1,0:T(2,128)(2,1)} %reshape.89), calls=%async_computation.1 | async-start | bytes 262144 | tf_op jit(solution)/shard_map/all_to_all | solution.py:148
  237.4 60.5 %copy-start.4 = (bf16[4,16,1024]{2,1,0:T(8,128)(2,1)S(1)}, bf16[4,16,1024]{2,1,0:T(8,128)(2,1)}, u32[]{:S(2)}) copy-start(bf16[4,16,1024]{2,1,0:T(8,128)(2,1)} %param.13) | copy-start | bytes 393220
  237.4 60.5 %all-to-all-start.2 = ((bf16[32,32,1024]{2,1,0:T(8,128)(2,1)}), bf16[32,32,1024]{2,1,0:T(8,128)(2,1)S(1)}, u32[]{:S(2)}, u32[]{:S(2)}) async-start(bf16[32,32,1024]{2,1,0:T(8,128)(2,1)} %stack.2), calls=%async_computation.2 | async-start | bytes 4194304 | tf_op jit(solution)/shard_map/all_to_all | solution.py:159
  249.6 49.4 %copy-start.3 = (f32[128,128]{1,0:T(8,128)}, f32[128,128]{1,0:T(8,128)S(1)}, u32[]{:S(2)}) copy-start(f32[128,128]{1,0:T(8,128)S(1)} %fusion.13) | copy-start | bytes 196612
